TPU v7x, 32 devices: a whole 2x2x4 slice. The times are simulated.
32 devices in a mesh: dp: 8 (over z, x), mp: 4 (over y, core).
Axes of the slice: x: 2, y: 2, z: 4, core: 2. Of those that a mesh axis runs over, the one named last changes fastest.
Arguments:
- hidden_in: bfloat16 [8, 2048, 960], P('dp', 'mp'), may hold values from -6 to 6
- cotangent: bfloat16 [8, 2048, 960], P('dp', 'mp'), may hold values from -6 to 6
- segments: int32 [8, 2048], P('dp'), may hold values from 0 to 3, never falling along the last dimension, each value on 1 to 1024 neighbouring positions
- positions: int32 [8, 2048], P('dp', 'mp'), may hold values from 0 to 4095
- attn_in: bfloat16 [960, 1600], P('dp', 'mp'), may hold values from -0.1875 to 0.1875
- attn_out: bfloat16 [960, 960], P('mp', 'dp'), may hold values from -0.75 to 0.75
- w_gate: bfloat16 [960, 2560], P('dp', 'mp'), may hold values from -0.1875 to 0.1875
- w_up: bfloat16 [960, 2560], P('dp', 'mp'), may hold values from -0.1875 to 0.1875
- w_down: bfloat16 [2560, 960], P('mp', 'dp'), may hold values from -0.125 to 0.125
- norm1_gain: bfloat16 [960], P('dp'), may hold values from 0.099609375 to 1.8984375
- norm2_gain: bfloat16 [960], P('dp'), may hold values from 0.099609375 to 1.8984375
Outputs:
- hidden_out: bfloat16 [8, 2048, 960], P('dp', 'mp')
- grad_hidden: float32 [8, 2048, 960], P('dp', 'mp')
- grad_attn_in: float32 [960, 1600], P('dp', 'mp')
- grad_attn_out: float32 [960, 960], P('mp', 'dp')
- grad_gate: float32 [960, 2560], P('dp', 'mp')
- grad_up: float32 [960, 2560], P('dp', 'mp')
- grad_down: float32 [2560, 960], P('mp', 'dp')
- grad_gain1: float32 [960], P('dp')
- grad_gain2: float32 [960], P('dp')
Inputs may be any that keep to these rules, and one draw needn't show every extreme that they name: `segments`: segment numbers never fall along a sequence; every segment is a run of 1 to 1024 tokens.
All inputs are finite; a program needn't handle non-finite values.
Results may differ from a plain program's by a relative error of at most 0.015.
Values may be sent and summed in bfloat16 or wider, within the bound.
A program may use at most 192 MiB of HBM per device.

v0:
```python
import math
import jax
import jax.numpy as jnp
from jax import lax
from jax.sharding import PartitionSpec as P

HEADS = 15
KV_HEADS = 5
HEAD_DIM = 64
EPSILON = 1e-05
SCORE_SCALE = 0.125
MASK_FILL = -1e30


def rms_forward(values_in, gain):
    inverse = lax.rsqrt(jnp.mean(values_in * values_in, axis=-1, keepdims=True) + EPSILON)
    return (values_in * inverse * gain, inverse)


def rms_backward(values_in, inverse, gain, upstream):
    scaled = upstream * gain
    grad_in = inverse * (
        scaled
        - values_in * inverse * inverse * jnp.mean(scaled * values_in, axis=-1, keepdims=True)
    )
    return (grad_in, jnp.sum(upstream * values_in * inverse, axis=0))


def rotary_tables(position_ids):
    half_dim = HEAD_DIM // 2
    frequency = jnp.exp(
        jnp.arange(half_dim, dtype=jnp.float32) * (-2.0 * math.log(10000.0) / HEAD_DIM)
    )
    angles = position_ids.astype(jnp.float32)[:, None] * frequency[None, :]
    return (jnp.cos(angles)[:, None, :], jnp.sin(angles)[:, None, :])


def rotate(tensor, cosine, sine):
    half_dim = HEAD_DIM // 2
    first, second = (tensor[..., :half_dim], tensor[..., half_dim:])
    return jnp.concatenate(
        [first * cosine - second * sine, second * cosine + first * sine], axis=-1
    )


def rotate_back(tensor, cosine, sine):
    half_dim = HEAD_DIM // 2
    first, second = (tensor[..., :half_dim], tensor[..., half_dim:])
    return jnp.concatenate(
        [first * cosine + second * sine, second * cosine - first * sine], axis=-1
    )


def score_block(queries, keys, allowed):
    scores = (
        jnp.einsum("grd,sd->grs", queries, keys, preferred_element_type=jnp.float32) * SCORE_SCALE
    )
    return jnp.where(allowed[None], scores, MASK_FILL)


def attend(queries, keys, values, allowed):
    scores = score_block(queries, keys, allowed)
    peak = jnp.max(scores, axis=-1, keepdims=True)
    total = jnp.sum(jnp.exp(scores - peak), axis=-1, keepdims=True)
    log_total = peak + jnp.log(total)
    probs = jnp.exp(scores - log_total).astype(jnp.bfloat16)
    output = jnp.einsum("grs,sd->grd", probs, values, preferred_element_type=jnp.float32)
    return (output, log_total[..., 0])


def attend_back(queries, keys, values, allowed, log_total, output_b, grad_out_b):
    scores = score_block(queries, keys, allowed)
    probs = jnp.exp(scores - log_total[..., None])
    probs_b = probs.astype(jnp.bfloat16)
    grad_probs = jnp.einsum("grd,sd->grs", grad_out_b, values, preferred_element_type=jnp.float32)
    delta = jnp.sum(
        grad_out_b.astype(jnp.float32) * output_b.astype(jnp.float32), axis=-1, keepdims=True
    )
    grad_scores = (probs * (grad_probs - delta)).astype(jnp.bfloat16)
    grad_q = (
        jnp.einsum("grs,sd->grd", grad_scores, keys, preferred_element_type=jnp.float32)
        * SCORE_SCALE
    )
    grad_k = (
        jnp.einsum("grs,grd->sd", grad_scores, queries, preferred_element_type=jnp.float32)
        * SCORE_SCALE
    )
    grad_v = jnp.einsum("grs,grd->sd", probs_b, grad_out_b, preferred_element_type=jnp.float32)
    return (grad_q, grad_k, grad_v)


def per_device(
    hidden_in,
    cotangent,
    segments,
    positions,
    attn_in,
    attn_out,
    w_gate,
    w_up,
    w_down,
    norm1_gain,
    norm2_gain,
):
    tok_rows = hidden_in.shape[1]
    model_size = lax.axis_size("mp")
    seq_rows = tok_rows * model_size
    model_rank = lax.axis_index("mp")
    group_size = HEADS // KV_HEADS
    query_cols = HEADS * HEAD_DIM
    kv_cols = KV_HEADS * HEAD_DIM
    gathered = (
        lax.all_gather(attn_in, "dp", axis=0, tiled=True),
        lax.all_gather(attn_out, "dp", axis=1, tiled=True),
        lax.all_gather(w_gate, "dp", axis=0, tiled=True),
        lax.all_gather(w_up, "dp", axis=0, tiled=True),
        lax.all_gather(w_down, "dp", axis=1, tiled=True),
        lax.all_gather(norm1_gain, "dp", axis=0, tiled=True),
        lax.all_gather(norm2_gain, "dp", axis=0, tiled=True),
    )
    qkv_weight, out_weight = (
        lax.all_gather(gathered[0], "mp", axis=1, tiled=True),
        lax.all_gather(gathered[1], "mp", axis=0, tiled=True),
    )
    gate_weight, up_weight, down_weight = (gathered[2], gathered[3], gathered[4])
    gain_one = gathered[5].astype(jnp.float32)
    gain_two = gathered[6].astype(jnp.float32)
    resid_in = hidden_in[0].astype(jnp.float32)
    normed1, inv_one = rms_forward(resid_in, gain_one)
    normed1_b = normed1.astype(jnp.bfloat16)
    projected = jnp.dot(normed1_b, qkv_weight, preferred_element_type=jnp.float32)
    cosine, sine = rotary_tables(positions[0])
    queries = rotate(
        projected[:, :query_cols].reshape(tok_rows, HEADS, HEAD_DIM), cosine, sine
    ).astype(jnp.bfloat16)
    keys_own = (
        rotate(
            projected[:, query_cols : query_cols + kv_cols].reshape(tok_rows, KV_HEADS, HEAD_DIM),
            cosine,
            sine,
        )
        .astype(jnp.bfloat16)
        .reshape(tok_rows, kv_cols)
    )
    values_own = projected[:, query_cols + kv_cols :].astype(jnp.bfloat16)
    keys_all, values_all = (
        lax.all_gather(keys_own, "mp", axis=0, tiled=True),
        lax.all_gather(values_own, "mp", axis=0, tiled=True),
    )
    seq_seg = segments[0]
    query_seg = lax.dynamic_slice_in_dim(seq_seg, model_rank * tok_rows, tok_rows, 0)
    query_index = model_rank * tok_rows + jnp.arange(tok_rows, dtype=jnp.int32)
    key_index = jnp.arange(seq_rows, dtype=jnp.int32)
    allowed = (query_seg[:, None] == seq_seg[None, :]) & (
        key_index[None, :] <= query_index[:, None]
    )
    query_groups = queries.reshape(tok_rows, KV_HEADS, group_size, HEAD_DIM).transpose(1, 2, 0, 3)
    key_groups = keys_all.reshape(seq_rows, KV_HEADS, HEAD_DIM).transpose(1, 0, 2)
    value_groups = values_all.reshape(seq_rows, KV_HEADS, HEAD_DIM).transpose(1, 0, 2)
    outputs, log_totals = lax.map(
        lambda pack: attend(pack[0], pack[1], pack[2], allowed),
        (query_groups, key_groups, value_groups),
    )
    out_groups = outputs.astype(jnp.bfloat16)
    attn_b = out_groups.transpose(2, 0, 1, 3).reshape(tok_rows, query_cols)
    middle = resid_in + jnp.dot(attn_b, out_weight, preferred_element_type=jnp.float32)
    normed2, inv_two = rms_forward(middle, gain_two)
    normed2_b = normed2.astype(jnp.bfloat16)
    seq_normed = lax.all_gather(normed2_b, "mp", axis=0, tiled=True)
    gate = jnp.dot(seq_normed, gate_weight, preferred_element_type=jnp.float32)
    upper = jnp.dot(seq_normed, up_weight, preferred_element_type=jnp.float32)
    sigma = jax.nn.sigmoid(gate)
    silu_gate = gate * sigma
    hidden_b = (silu_gate * upper).astype(jnp.bfloat16)
    ffn_out = lax.psum_scatter(
        jnp.dot(hidden_b, down_weight, preferred_element_type=jnp.float32).astype(jnp.bfloat16),
        "mp",
        scatter_dimension=0,
        tiled=True,
    ).astype(jnp.float32)
    hidden_out = (middle + ffn_out).astype(jnp.bfloat16)
    regathered = (
        lax.all_gather(attn_in, "dp", axis=0, tiled=True),
        lax.all_gather(attn_out, "dp", axis=1, tiled=True),
        lax.all_gather(w_gate, "dp", axis=0, tiled=True),
        lax.all_gather(w_up, "dp", axis=0, tiled=True),
        lax.all_gather(w_down, "dp", axis=1, tiled=True),
        lax.all_gather(norm1_gain, "dp", axis=0, tiled=True),
        lax.all_gather(norm2_gain, "dp", axis=0, tiled=True),
    )
    qkv_weight, out_weight = (
        lax.all_gather(regathered[0], "mp", axis=1, tiled=True),
        lax.all_gather(regathered[1], "mp", axis=0, tiled=True),
    )
    gate_weight, up_weight, down_weight = (regathered[2], regathered[3], regathered[4])
    gain_one = regathered[5].astype(jnp.float32)
    gain_two = regathered[6].astype(jnp.float32)
    cot_local = cotangent[0]
    seq_cot = lax.all_gather(cot_local, "mp", axis=0, tiled=True)
    g_down = jnp.dot(hidden_b.T, seq_cot, preferred_element_type=jnp.float32)
    grad_hid = jnp.dot(seq_cot, down_weight.T, preferred_element_type=jnp.float32)
    grad_gate_act = (grad_hid * upper * sigma * (1.0 + gate * (1.0 - sigma))).astype(jnp.bfloat16)
    grad_up_act = (grad_hid * silu_gate).astype(jnp.bfloat16)
    g_gate = jnp.dot(seq_normed.T, grad_gate_act, preferred_element_type=jnp.float32)
    g_up = jnp.dot(seq_normed.T, grad_up_act, preferred_element_type=jnp.float32)
    grad_norm2 = lax.psum_scatter(
        jnp.dot(grad_gate_act, gate_weight.T, preferred_element_type=jnp.float32)
        + jnp.dot(grad_up_act, up_weight.T, preferred_element_type=jnp.float32),
        "mp",
        scatter_dimension=0,
        tiled=True,
    )
    grad_mid_norm, g_gain2 = rms_backward(middle, inv_two, gain_two, grad_norm2)
    grad_middle = cot_local.astype(jnp.float32) + grad_mid_norm
    middle_b = grad_middle.astype(jnp.bfloat16)
    g_out = jnp.dot(attn_b.T, middle_b, preferred_element_type=jnp.float32)
    grad_attn_b = jnp.dot(middle_b, out_weight.T, preferred_element_type=jnp.float32).astype(
        jnp.bfloat16
    )
    grad_groups = grad_attn_b.reshape(tok_rows, KV_HEADS, group_size, HEAD_DIM).transpose(
        1, 2, 0, 3
    )
    grad_q, grad_k, grad_v = lax.map(
        lambda pack: attend_back(pack[0], pack[1], pack[2], allowed, pack[3], pack[4], pack[5]),
        (query_groups, key_groups, value_groups, log_totals, out_groups, grad_groups),
    )
    key_grads, value_grads = (
        lax.psum_scatter(grad_k, "mp", scatter_dimension=1, tiled=True),
        lax.psum_scatter(grad_v, "mp", scatter_dimension=1, tiled=True),
    )
    grad_q = rotate_back(
        grad_q.transpose(2, 0, 1, 3).reshape(tok_rows, HEADS, HEAD_DIM), cosine, sine
    )
    key_grads = rotate_back(key_grads.transpose(1, 0, 2), cosine, sine)
    value_grads = value_grads.transpose(1, 0, 2)
    grad_proj = jnp.concatenate(
        [
            grad_q.reshape(tok_rows, query_cols),
            key_grads.reshape(tok_rows, kv_cols),
            value_grads.reshape(tok_rows, kv_cols),
        ],
        axis=1,
    ).astype(jnp.bfloat16)
    g_in = jnp.dot(normed1_b.T, grad_proj, preferred_element_type=jnp.float32)
    grad_norm1 = jnp.dot(grad_proj, qkv_weight.T, preferred_element_type=jnp.float32)
    grad_in_norm, g_gain1 = rms_backward(resid_in, inv_one, gain_one, grad_norm1)
    grad_input = grad_middle + grad_in_norm
    reduced = (
        lax.psum_scatter(g_in, "dp", scatter_dimension=0, tiled=True),
        lax.psum_scatter(g_out, "dp", scatter_dimension=1, tiled=True),
        lax.psum_scatter(g_gate, "dp", scatter_dimension=0, tiled=True),
        lax.psum_scatter(g_up, "dp", scatter_dimension=0, tiled=True),
        lax.psum_scatter(g_down, "dp", scatter_dimension=1, tiled=True),
        lax.psum_scatter(g_gain1, "dp", scatter_dimension=0, tiled=True),
        lax.psum_scatter(g_gain2, "dp", scatter_dimension=0, tiled=True),
    )
    grad_attn_in, grad_attn_out = (
        lax.psum_scatter(reduced[0], "mp", scatter_dimension=1, tiled=True),
        lax.psum_scatter(reduced[1], "mp", scatter_dimension=0, tiled=True),
    )
    grad_gain1, grad_gain2 = lax.psum((reduced[5], reduced[6]), "mp")
    return (
        hidden_out[None],
        grad_input[None],
        grad_attn_in,
        grad_attn_out,
        reduced[2],
        reduced[3],
        reduced[4],
        grad_gain1,
        grad_gain2,
    )


def solution(mesh):
    return jax.shard_map(
        per_device,
        mesh=mesh,
        in_specs=(
            P("dp", "mp", None),
            P("dp", "mp", None),
            P("dp", None),
            P("dp", "mp"),
            P("dp", "mp"),
            P("mp", "dp"),
            P("dp", "mp"),
            P("dp", "mp"),
            P("mp", "dp"),
            P("dp"),
            P("dp"),
        ),
        out_specs=(
            P("dp", "mp", None),
            P("dp", "mp", None),
            P("dp", "mp"),
            P("mp", "dp"),
            P("dp", "mp"),
            P("dp", "mp"),
            P("mp", "dp"),
            P("dp"),
            P("dp"),
        ),
        check_vma=False,
    )
```

profile of v0, /device:TPU:0, one launch (start us, length us, event | category | flops | bytes accessed | tf_op | source)
XLA Modules:
  0.0 1195.8 jit_solution(7193035129277229926)
XLA Ops:
  7.3 34.3 %all-gather.1 = bf16[8,120,400]{1,2,0:T(8,128)(2,1)S(1)} all-gather(bf16[1,120,400]{1,2,0:T(8,128)(2,1)} %bitcast.241), channel_id=1, replica_groups=mesh['dp'=8,'mp'=4] {'dp'}, dimensions={0}, use_global_device_ids=true | all-gather | bytes 864000 | tf_op jit(solution)/shard_map/all_gather | solution.py:113
  45.2 21.3 %all-reduce.10 = (bf16[960]{0:T(1024)(128)(2,1)S(1)}, bf16[960]{0:T(1024)(128)(2,1)S(1)}) all-reduce(bf16[960]{0:T(1024)(128)(2,1)S(1)} %dynamic-update-slice, bf16[960]{0:T(1024)(128)(2,1)S(1)} %dynamic-update-slice.1), channel_id=1, replica_groups=mesh['dp'=8,'mp'=4] {'dp'}, use_global_device_ids=true, to_apply=%add | all-reduce | flops 1920 | bytes 7680
  80.2 33.2 %all_gather.53 = bf16[240,960]{0,1:T(8,128)(2,1)} all-gather(bf16[240,120]{0,1:T(8,128)(2,1)S(1)} %copy.27), channel_id=1, replica_groups=mesh['dp'=8,'mp'=4] {'dp'}, dimensions={1}, use_global_device_ids=true | all-gather | bytes 518400 | tf_op jit(solution)/shard_map/all_gather | solution.py:114
  117.5 114.8 %while.30 = (s32[]{:T(128)}, bf16[5,3,512,64]{2,3,1,0:T(8,128)(2,1)S(1)}, f32[5,3,512]{2,1,0:T(4,128)S(1)}, bf16[5,3,512,64]{2,3,1,0:T(8,128)(2,1)S(1)}, bf16[5,...) while((s32[]{:T(128)}, ...), condition=%wide.region_4.5_spmd.clone.clone, body=%wide.region_1.4_spmd.clone.sunk.clone | while | flops 843053568 | bytes 43130984 | solution.py:160
  240.1 30.8 %all-gather.20.cloned.1.call-done = bf16[2048,960]{0,1:T(8,128)(2,1)} async-done(((bf16[512,960]{0,1:T(8,128)(2,1)}), bf16[2048,960]{0,1:T(8,128)(2,1)}) %all-gather.20.cloned.1.call-update) | async-done | bytes 3932176 | tf_op jit(solution)/shard_map/all_gather | solution.py:169
  270.9 8.3 fusion.89
  279.2 35.4 %all-gather.22.cloned.1.call-done = bf16[960,640]{1,0:T(8,128)(2,1)} async-done(((bf16[120,640]{1,0:T(8,128)(2,1)}), bf16[960,640]{1,0:T(8,128)(2,1)}) %all-gather.22.cloned.1.call-update) | async-done | bytes 1228816 | tf_op jit(solution)/shard_map/all_gather | solution.py:115
  314.6 8.3 fusion.88
  322.9 34.1 %all-gather.26.cloned.1.call-done = bf16[640,960]{0,1:T(8,128)(2,1)} async-done(((bf16[640,120]{0,1:T(8,128)(2,1)}), bf16[640,960]{0,1:T(8,128)(2,1)}) %all-gather.26.cloned.1.call-update) | async-done | bytes 1228816 | tf_op jit(solution)/shard_map/all_gather | solution.py:117
  357.0 33.4 %all-gather.28.cloned.1.call-done = bf16[1,2048,960]{1,2,0:T(8,128)(2,1)} async-done(((bf16[1,512,960]{1,2,0:T(8,128)(2,1)}), bf16[1,2048,960]{1,2,0:T(8,128)(2,1)}) %all-gather.28.cloned.1.call-update) | async-done | bytes 3932176 | tf_op jit(solution)/shard_map/all_gather | solution.py:199
  390.4 12.7 %multiply_convert_fusion.1 = (bf16[2048,640]{1,0:T(8,128)(2,1)S(1)}, bf16[2048,640]{1,0:T(8,128)(2,1)S(1)}, bf16[2048,640]{1,0:T(8,128)(2,1)}) fusion(f32[2048,640]{1,0:T(8,128)} %fusion.88, f32[2048,640]{1,0:T(8,128)} %fusion.89, bf16[640,960]{0,1:T(8,128)(2,1)} %all-gather.26.cloned.1.call-done, bf16[1,2048,960]{1,2,0:T(8,128)(2,1)} %all-gather.28.cloned.1.call-done), kind=kOutput, calls=%fused_computation.66 | convolution fusion | flops 2536243200 | bytes 23511040 | tf_op jit(solution)/shard_map/dot_general | solution.py:201
  419.3 61.8 %reduce-scatter.26.cloned.1.call-done = f32[512,960]{0,1:T(8,128)} async-done(((f32[2048,960]{0,1:T(8,128)}), f32[512,960]{0,1:T(8,128)}) %reduce-scatter.26.cloned.1.call-update) | async-done | bytes 1966096 | tf_op jit(solution)/shard_map/reduce_scatter | solution.py:206
  483.8 42.9 %reduce-scatter.24.cloned.1.call-done = bf16[512,960]{0,1:T(8,128)(2,1)} async-done(((bf16[2048,960]{0,1:T(8,128)(2,1)}), bf16[512,960]{0,1:T(8,128)(2,1)}) %reduce-scatter.24.cloned.1.call-update) | async-done | bytes 983056 | tf_op jit(solution)/shard_map/reduce_scatter | solution.py:175
  531.9 101.6 %while.31 = (s32[]{:T(128)}, f32[5,3,512,64]{2,3,1,0:T(8,128)}, f32[5,2048,64]{1,2,0:T(8,128)}, f32[5,2048,64]{1,2,0:T(8,128)}, bf16[5,3,512,64]{2,3,1,0:T(8,128...) while((s32[]{:T(128)}, f32[5,3,512,64]{2,3,1,0:T(8,128)}, ...), condition=%wide.region_11.12_spmd.clone.clone, body=%wide.region_9.11_spmd.clone.sunk.clone | while | flops 2048489984 | bytes 63237260 | solution.py:223
  641.9 26.4 %reduce-scatter.30.cloned.1.call-done = f32[5,512,64]{1,2,0:T(8,128)} async-done(((f32[5,2048,64]{1,2,0:T(8,128)}), f32[5,512,64]{1,2,0:T(8,128)}) %reduce-scatter.30.cloned.1.call-update) | async-done | bytes 655376 | tf_op jit(solution)/shard_map/reduce_scatter | solution.py:229
  670.2 35.5 %reduce-scatter.28.cloned.1.call-done = f32[5,512,64]{1,2,0:T(8,128)} async-done(((f32[5,2048,64]{1,2,0:T(8,128)}), f32[5,512,64]{1,2,0:T(8,128)}) %reduce-scatter.28.cloned.1.call-update) | async-done | bytes 655376 | tf_op jit(solution)/shard_map/reduce_scatter | solution.py:228
  736.1 57.5 %reduce-scatter.36.cloned.1.call-done = f32[120,960]{1,0:T(8,128)} async-done(((f32[960,960]{1,0:T(8,128)}), f32[120,960]{1,0:T(8,128)}) %reduce-scatter.36.cloned.1.call-update) | async-done | bytes 460816
  796.0 122.4 %reduce-scatter.38.cloned.1.call-done = f32[120,1600]{1,0:T(8,128)} async-done(((f32[960,1600]{1,0:T(8,128)}), f32[120,1600]{1,0:T(8,128)}) %reduce-scatter.38.cloned.1.call-update) | async-done | bytes 768016
  927.2 20.1 %all-reduce.8 = (f32[960]{0:T(1024)S(1)}, f32[960]{0:T(1024)S(1)}) all-reduce(f32[960]{0:T(1024)S(1)} %get-tuple-element.203, f32[960]{0:T(1024)S(1)} %copy-done.14), channel_id=14, replica_groups=mesh['dp'=8,'mp'=4] {'dp'}, use_global_device_ids=true, to_apply=%region_23.24.clone | all-reduce | flops 1920 | bytes 15360
  957.3 34.7 %reduce-scatter.44.cloned.1.call-done = f32[640,120]{0,1:T(8,128)} async-done(((f32[640,960]{0,1:T(8,128)}), f32[640,120]{0,1:T(8,128)}) %reduce-scatter.44.cloned.1.call-update) | async-done | bytes 307216
  992.0 73.3 %reduce-scatter.40.cloned.1.call-done = f32[120,640]{1,0:T(8,128)} async-done(((f32[960,640]{1,0:T(8,128)}), f32[120,640]{1,0:T(8,128)}) %reduce-scatter.40.cloned.1.call-update) | async-done | bytes 307216
  1065.3 73.2 %reduce-scatter.42.cloned.1.call-done = f32[120,640]{1,0:T(8,128)} async-done(((f32[960,640]{1,0:T(8,128)}), f32[120,640]{1,0:T(8,128)}) %reduce-scatter.42.cloned.1.call-update) | async-done | bytes 307216
  1138.5 23.6 %reduce-scatter.32.cloned.1.call-done = f32[240,120]{1,0:T(8,128)} async-done(((f32[960,120]{1,0:T(8,128)}), f32[240,120]{1,0:T(8,128)}) %reduce-scatter.32.cloned.1.call-update) | async-done | bytes 115216 | tf_op jit(solution)/shard_map/reduce_scatter | solution.py:259
  1162.1 26.6 %reduce-scatter.34.cloned.1.call-done = f32[400,120]{1,0:T(8,128)} async-done(((f32[1600,120]{1,0:T(8,128)}), f32[400,120]{1,0:T(8,128)}) %reduce-scatter.34.cloned.1.call-update) | async-done | bytes 192016
  (222 shorter events, 329.0 us)
Async XLA Ops:
  7.2 59.3 %copy-start.5 = (bf16[1,512,960]{1,2,0:T(8,128)(2,1)S(1)}, bf16[1,512,960]{1,2,0:T(8,128)(2,1)}, u32[]{:S(2)}) copy-start(bf16[1,512,960]{1,2,0:T(8,128)(2,1)} %param.15) | copy-start | bytes 2949124
  7.2 66.5 %all-gather.12.cloned.1.call-start = ((), (), s32[]{:S(2)}) async-start(), calls=%async_computation.11 | async-start | bytes 4096000 | tf_op jit(solution)/shard_map/all_gather | solution.py:122
  43.4 74.1 %all-gather.16.cloned.1.call-start = ((), (), s32[]{:S(2)}) async-start(), calls=%async_computation.13 | async-start | bytes 1638400 | tf_op jit(solution)/shard_map/all_gather | solution.py:148
  78.7 38.8 %all-gather.14.cloned.1.call-start = ((), (), s32[]{:S(2)}) async-start(), calls=%async_computation.12 | async-start | bytes 1638400 | tf_op jit(solution)/shard_map/all_gather | solution.py:147
  80.1 152.3 %all-gather.18.cloned.1.call-start = ((), (), s32[]{:S(2)}) async-start(), calls=%async_computation.14 | async-start | bytes 2457600 | tf_op jit(solution)/shard_map/all_gather | solution.py:123
  115.5 124.6 %all-gather.24.cloned.1.call-start = ((), (), s32[]{:S(2)}) async-start(), calls=%async_computation.17 | async-start | bytes 1382400 | tf_op jit(solution)/shard_map/all_gather | solution.py:116
  116.1 154.8 %all-gather.20.cloned.1.call-start = ((), (), s32[]{:S(2)}) async-start(), calls=%async_computation.15 | async-start | bytes 4915200 | tf_op jit(solution)/shard_map/all_gather | solution.py:169
  237.5 77.0 %all-gather.22.cloned.1.call-start = ((), (), s32[]{:S(2)}) async-start(), calls=%async_computation.16 | async-start | bytes 1382400 | tf_op jit(solution)/shard_map/all_gather | solution.py:115
  238.3 118.7 %all-gather.26.cloned.1.call-start = ((), (), s32[]{:S(2)}) async-start(), calls=%async_computation.18 | async-start | bytes 1382400 | tf_op jit(solution)/shard_map/all_gather | solution.py:117
  239.1 151.4 %all-gather.28.cloned.1.call-start = ((), (), s32[]{:S(2)}) async-start(), calls=%async_computation.24 | async-start | bytes 4915200 | tf_op jit(solution)/shard_map/all_gather | solution.py:199
  239.8 241.3 %reduce-scatter.26.cloned.1.call-start = ((), (), s32[]{:S(2)}) async-start(), calls=%async_computation.20 | async-start | bytes 9830400 | tf_op jit(solution)/shard_map/reduce_scatter | solution.py:206
  412.0 114.8 %reduce-scatter.24.cloned.1.call-start = ((), (), s32[]{:S(2)}) async-start(), calls=%async_computation.19 | async-start | bytes 4915200 | tf_op jit(solution)/shard_map/reduce_scatter | solution.py:175
  419.2 249.1 %reduce-scatter.30.cloned.1.call-start = ((), (), s32[]{:S(2)}) async-start(), calls=%async_computation.22 | async-start | bytes 3276800 | tf_op jit(solution)/shard_map/reduce_scatter | solution.py:229
  633.5 72.2 %reduce-scatter.28.cloned.1.call-start = ((), (), s32[]{:S(2)}) async-start(), calls=%async_computation.21 | async-start | bytes 3276800 | tf_op jit(solution)/shard_map/reduce_scatter | solution.py:228
  634.2 159.4 %reduce-scatter.36.cloned.1.call-start = ((), (), s32[]{:S(2)}) async-start(), calls=%async_computation.26 | async-start | bytes 4423680
  638.2 280.3 %reduce-scatter.38.cloned.1.call-start = ((), (), s32[]{:S(2)}) async-start(), calls=%async_computation.27 | async-start | bytes 7188480
  640.9 66.1 %copy-start.6 = (bf16[1,512,960]{1,2,0:T(8,128)(2,1)S(1)}, bf16[1,512,960]{1,2,0:T(8,128)(2,1)}, u32[]{:S(2)}) copy-start(bf16[1,512,960]{1,2,0:T(8,128)(2,1)} %param.15) | copy-start | bytes 2949124
  640.9 66.1 %copy-start.16 = (f32[960]{0:T(1024)S(1)}, f32[960]{0:T(1024)}, u32[]{:S(2)}) copy-start(f32[960]{0:T(1024)} %copy-done.15) | copy-start | bytes 11524
  640.9 66.1 %copy-start.18 = (f32[512]{0:T(512)S(1)}, f32[512]{0:T(512)}, u32[]{:S(2)}) copy-start(f32[512]{0:T(512)} %copy-done.17) | copy-start | bytes 6148
  713.0 279.0 %reduce-scatter.44.cloned.1.call-start = ((), (), s32[]{:S(2)}) async-start(), calls=%async_computation.30 | async-start | bytes 2764800
  720.6 344.7 %reduce-scatter.40.cloned.1.call-start = ((), (), s32[]{:S(2)}) async-start(), calls=%async_computation.28 | async-start | bytes 2764800
  728.3 410.2 %reduce-scatter.42.cloned.1.call-start = ((), (), s32[]{:S(2)}) async-start(), calls=%async_computation.29 | async-start | bytes 2764800
  736.0 426.0 %reduce-scatter.32.cloned.1.call-start = ((), (), s32[]{:S(2)}) async-start(), calls=%async_computation.23 | async-start | bytes 614400 | tf_op jit(solution)/shard_map/reduce_scatter | solution.py:259
  795.7 393.0 %reduce-scatter.34.cloned.1.call-start = ((), (), s32[]{:S(2)}) async-start(), calls=%async_computation.25 | async-start | bytes 1024000
  (23 other events, 337.1 us)
Sparse Core Ops, SparseCore 0:
  43.5 30.1 all-gather.11
  78.8 18.1 all-gather.15
  99.2 18.1 all-gather.13
  119.4 21.8 all-gather.17
  143.3 41.4 all-gather.23
  237.7 33.2 all-gather.19
  273.1 41.4 all-gather.21
  316.8 40.2 all-gather.25
  358.6 31.7 all-gather.27
  412.1 68.9 reduce-scatter.25
  483.8 42.8 reduce-scatter.23
  633.6 34.6 reduce-scatter.29
  671.0 34.6 reduce-scatter.27
  709.3 84.3 reduce-scatter.35
  797.5 120.8 reduce-scatter.37
  922.9 69.0 reduce-scatter.43
  996.5 68.8 reduce-scatter.39
  1069.8 68.6 reduce-scatter.41
  1141.7 20.2 reduce-scatter.31
  1165.2 23.4 reduce-scatter.33
where the time goes:
time: 1200 us
  waiting for transfers between devices  722 us (60%)
  matrix products  261 us (22%)
  blocking collectives  115 us (10%)
  other arithmetic  65.6 us (5%)
  between operations  16.4 us (1%)
  local copies, waits for them, and re-layouts  13.4 us (1%)
    unnamed x26, waiting for transfers between devices  391 us
    reduce_scatter x1, waiting for transfers between devices, per_device(): lax.psum_scatter(jnp.dot(grad_gate_act, gate_weight.T, preferred_element_...  61.8 us
    dot_general x10, matrix products, score_block(): jnp.einsum('grd,sd->grs', queries, keys, preferred_element_type=jnp.float32)  48.5 us
    reduce_scatter x1, waiting for transfers between devices, per_device(): lax.psum_scatter(jnp.dot(hidden_b, down_weight, preferred_element_type=jn...  42.9 us
    unnamed x2, blocking collectives  41.4 us
    dot_general x5, matrix products, attend(): jnp.einsum('grs,sd->grd', probs, values, preferred_element_type=jnp.float32)  40.2 us
    reduce_scatter x1, waiting for transfers between devices, per_device(): lax.psum_scatter(grad_k, 'mp', scatter_dimension=1, tiled=True)  35.5 us
    all_gather x1, waiting for transfers between devices, per_device(): lax.all_gather(w_gate, 'dp', axis=0, tiled=True)  35.4 us
  transfers between devices with their start and end apart: 20, of which 16 were waited for; matrix products, arithmetic and copies ran while one was open for 17% of the time, Pallas kernels for 0%

commit v1 on v0

--- a/solution.py
+++ b/solution.py
@@ -10,6 +10,27 @@
 EPSILON = 1e-05
 SCORE_SCALE = 0.125
 MASK_FILL = -1e30
+
+
+def gather_around(x, axis, dim):
+    devices, index, span = (lax.axis_size(axis), lax.axis_index(axis), x.shape[dim])
+    right = [(i, (i + 1) % devices) for i in range(devices)]
+    left = [(i, (i - 1) % devices) for i in range(devices)]
+    filled = jnp.zeros((*x.shape[:dim], devices * span, *x.shape[dim + 1 :]), x.dtype)
+    filled = lax.dynamic_update_slice_in_dim(filled, x, index * span, axis=dim)
+    from_left = from_right = x
+    half = devices // 2
+    for lap in range(1, half + 1):
+        from_left = lax.ppermute(from_left, axis, right)
+        filled = lax.dynamic_update_slice_in_dim(
+            filled, from_left, (index - lap) % devices * span, axis=dim
+        )
+        if lap < devices - half:
+            from_right = lax.ppermute(from_right, axis, left)
+            filled = lax.dynamic_update_slice_in_dim(
+                filled, from_right, (index + lap) % devices * span, axis=dim
+            )
+    return filled
 
 
 def rms_forward(values_in, gain):
@@ -112,7 +133,7 @@
     gathered = (
         lax.all_gather(attn_in, "dp", axis=0, tiled=True),
         lax.all_gather(attn_out, "dp", axis=1, tiled=True),
-        lax.all_gather(w_gate, "dp", axis=0, tiled=True),
+        gather_around(w_gate, "dp", 0),
         lax.all_gather(w_up, "dp", axis=0, tiled=True),
         lax.all_gather(w_down, "dp", axis=1, tiled=True),
         lax.all_gather(norm1_gain, "dp", axis=0, tiled=True),

time: 1200 us -> 1150 us (0.958)
  waiting for transfers between devices: 722 us -> 649 us
  starting transfers between devices: 1.66 us -> 17.2 us
    all_gather x1, waiting for transfers between devices: 34.1 us -> 0.01 us  [per_device(): lax.all_gather(w_down, 'dp', axis=1, tiled=True)]
    all_gather x1, waiting for transfers between devices: 33.4 us -> 0.01 us  [per_device(): seq_cot = lax.all_gather(cot_local, 'mp', axis=0, tiled=True)]
    ppermute x0 -> x7, starting transfers between devices: none -> 15.8 us  [the longest x3 8.47 us: gather_around(): from_right = lax.ppermute(from_right, axis, left)]
    ppermute x0 -> x7, waiting for transfers between devices: none -> 14.1 us  [the longest x4 13.2 us: gather_around(): from_left = lax.ppermute(from_left, axis, right)]
  transfers between devices with their start and end apart: 20 -> 27, of which waited for: 16 -> 21; matrix products, arithmetic and copies ran while one was open for 17% -> 19% of each run, Pallas kernels for 0% -> 0%
where the time goes in v1:
time: 1150 us; the launch traced here: 1140 us
  waiting for transfers between devices  649 us (56%)
  matrix products  258 us (22%)
  blocking collectives  114 us (10%)
  other arithmetic  65.6 us (6%)
  local copies, waits for them, and re-layouts  23.3 us (2%)
  starting transfers between devices  17.2 us (1%)
  between operations  16.6 us (1%)
    unnamed x26, waiting for transfers between devices  390 us
    reduce_scatter x1, waiting for transfers between devices, per_device(): lax.psum_scatter(jnp.dot(grad_gate_act, gate_weight.T, preferred_element_...  60.6 us
    dot_general x10, matrix products, score_block(): jnp.einsum('grd,sd->grs', queries, keys, preferred_element_type=jnp.float32)  49.4 us
    reduce_scatter x1, waiting for transfers between devices, per_device(): lax.psum_scatter(jnp.dot(hidden_b, down_weight, preferred_element_type=jn...  42.9 us
    unnamed x2, blocking collectives  41.4 us
    dot_general x5, matrix products, attend(): jnp.einsum('grs,sd->grd', probs, values, preferred_element_type=jnp.float32)  40.4 us
    reduce_scatter x1, waiting for transfers between devices, per_device(): lax.psum_scatter(grad_k, 'mp', scatter_dimension=1, tiled=True)  35.6 us
    reduce_sum x5, other arithmetic, attend(): total = jnp.sum(jnp.exp(scores - peak), axis=-1, keepdims=True)  34.3 us
  transfers between devices with their start and end apart: 27, of which 21 were waited for; matrix products, arithmetic and copies ran while one was open for 19% of the time, Pallas kernels for 0%

profile of v1, /device:TPU:0, one launch (start us, length us, event | category | flops | bytes accessed | tf_op | source)
XLA Modules:
  0.0 1144.1 jit_solution(14545484000678571474)
XLA Ops:
  7.3 34.3 %all-gather.1 = bf16[8,120,400]{1,2,0:T(8,128)(2,1)S(1)} all-gather(bf16[1,120,400]{1,2,0:T(8,128)(2,1)} %bitcast.239), channel_id=1, replica_groups=mesh['dp'=8,'mp'=4] {'dp'}, dimensions={0}, use_global_device_ids=true | all-gather | bytes 864000 | tf_op jit(solution)/shard_map/all_gather | solution.py:134
  45.2 21.3 %all-reduce.10 = (bf16[960]{0:T(1024)(128)(2,1)S(1)}, bf16[960]{0:T(1024)(128)(2,1)S(1)}) all-reduce(bf16[960]{0:T(1024)(128)(2,1)S(1)} %dynamic-update-slice, bf16[960]{0:T(1024)(128)(2,1)S(1)} %dynamic-update-slice.1), channel_id=1, replica_groups=mesh['dp'=8,'mp'=4] {'dp'}, use_global_device_ids=true, to_apply=%add | all-reduce | flops 1920 | bytes 7680
  82.8 31.5 %all_gather.52 = bf16[240,960]{0,1:T(8,128)(2,1)S(1)} all-gather(bf16[240,120]{0,1:T(8,128)(2,1)S(1)} %copy.27), channel_id=1, replica_groups=mesh['dp'=8,'mp'=4] {'dp'}, dimensions={1}, use_global_device_ids=true | all-gather | bytes 518400 | tf_op jit(solution)/shard_map/all_gather | solution.py:135
  118.8 115.9 %while.30 = (s32[]{:T(128)}, bf16[5,3,512,64]{2,3,1,0:T(8,128)(2,1)S(1)}, f32[5,3,512]{2,1,0:T(4,128)S(1)}, bf16[5,3,512,64]{2,3,1,0:T(8,128)(2,1)S(1)}, bf16[5,...) while((s32[]{:T(128)}, ...), condition=%wide.region_4.5_spmd.clone.clone, body=%wide.region_1.4_spmd.clone.sunk.clone | while | flops 843053568 | bytes 43130984 | solution.py:181
  134.1 8.1 fusion.159
  203.6 8.1 fusion.159
  226.5 8.2 fusion.159
  278.5 8.7 fusion.63
  287.2 19.4 %all-gather.20.cloned.1.call-done = bf16[2048,960]{0,1:T(8,128)(2,1)} async-done(((bf16[512,960]{0,1:T(8,128)(2,1)}), bf16[2048,960]{0,1:T(8,128)(2,1)}) %all-gather.20.cloned.1.call-update) | async-done | bytes 3932176 | tf_op jit(solution)/shard_map/all_gather | solution.py:190
  312.8 9.1 multiply_convert_fusion.1
  321.8 28.5 %all-gather.26.cloned.1.call-done = bf16[960,640]{1,0:T(8,128)(2,1)} async-done(((bf16[120,640]{1,0:T(8,128)(2,1)}), bf16[960,640]{1,0:T(8,128)(2,1)}) %all-gather.26.cloned.1.call-update) | async-done | bytes 1228816 | tf_op jit(solution)/shard_map/all_gather | solution.py:206
  368.7 60.6 %reduce-scatter.26.cloned.1.call-done = f32[512,960]{0,1:T(8,128)} async-done(((f32[2048,960]{0,1:T(8,128)}), f32[512,960]{0,1:T(8,128)}) %reduce-scatter.26.cloned.1.call-update) | async-done | bytes 1966096 | tf_op jit(solution)/shard_map/reduce_scatter | solution.py:227
  432.0 42.9 %reduce-scatter.24.cloned.1.call-done = bf16[512,960]{0,1:T(8,128)(2,1)} async-done(((bf16[2048,960]{0,1:T(8,128)(2,1)}), bf16[512,960]{0,1:T(8,128)(2,1)}) %reduce-scatter.24.cloned.1.call-update) | async-done | bytes 983056 | tf_op jit(solution)/shard_map/reduce_scatter | solution.py:196
  480.0 101.7 %while.31 = (s32[]{:T(128)}, f32[5,3,512,64]{2,3,1,0:T(8,128)}, f32[5,2048,64]{1,2,0:T(8,128)}, f32[5,2048,64]{1,2,0:T(8,128)}, bf16[5,3,512,64]{2,3,1,0:T(8,128...) while((s32[]{:T(128)}, f32[5,3,512,64]{2,3,1,0:T(8,128)}, ...), condition=%wide.region_11.12_spmd.clone.clone, body=%wide.region_9.11_spmd.clone.sunk.clone | while | flops 2048489984 | bytes 63237260 | solution.py:244
  590.1 26.4 %reduce-scatter.30.cloned.1.call-done = f32[5,512,64]{1,2,0:T(8,128)} async-done(((f32[5,2048,64]{1,2,0:T(8,128)}), f32[5,512,64]{1,2,0:T(8,128)}) %reduce-scatter.30.cloned.1.call-update) | async-done | bytes 655376 | tf_op jit(solution)/shard_map/reduce_scatter | solution.py:250
  618.4 35.6 %reduce-scatter.28.cloned.1.call-done = f32[5,512,64]{1,2,0:T(8,128)} async-done(((f32[5,2048,64]{1,2,0:T(8,128)}), f32[5,512,64]{1,2,0:T(8,128)}) %reduce-scatter.28.cloned.1.call-update) | async-done | bytes 655376 | tf_op jit(solution)/shard_map/reduce_scatter | solution.py:249
  684.3 57.6 %reduce-scatter.36.cloned.1.call-done = f32[120,960]{1,0:T(8,128)} async-done(((f32[960,960]{1,0:T(8,128)}), f32[120,960]{1,0:T(8,128)}) %reduce-scatter.36.cloned.1.call-update) | async-done | bytes 460816
  744.3 122.4 %reduce-scatter.38.cloned.1.call-done = f32[120,1600]{1,0:T(8,128)} async-done(((f32[960,1600]{1,0:T(8,128)}), f32[120,1600]{1,0:T(8,128)}) %reduce-scatter.38.cloned.1.call-update) | async-done | bytes 768016
  875.4 20.1 %all-reduce.8 = (f32[960]{0:T(1024)S(1)}, f32[960]{0:T(1024)S(1)}) all-reduce(f32[960]{0:T(1024)S(1)} %get-tuple-element.203, f32[960]{0:T(1024)S(1)} %copy-done.16), channel_id=14, replica_groups=mesh['dp'=8,'mp'=4] {'dp'}, use_global_device_ids=true, to_apply=%region_23.24.clone | all-reduce | flops 1920 | bytes 15360
  905.6 34.8 %reduce-scatter.44.cloned.1.call-done = f32[640,120]{0,1:T(8,128)} async-done(((f32[640,960]{0,1:T(8,128)}), f32[640,120]{0,1:T(8,128)}) %reduce-scatter.44.cloned.1.call-update) | async-done | bytes 307216
  940.4 73.2 %reduce-scatter.40.cloned.1.call-done = f32[120,640]{1,0:T(8,128)} async-done(((f32[960,640]{1,0:T(8,128)}), f32[120,640]{1,0:T(8,128)}) %reduce-scatter.40.cloned.1.call-update) | async-done | bytes 307216
  1013.6 73.1 %reduce-scatter.42.cloned.1.call-done = f32[120,640]{1,0:T(8,128)} async-done(((f32[960,640]{1,0:T(8,128)}), f32[120,640]{1,0:T(8,128)}) %reduce-scatter.42.cloned.1.call-update) | async-done | bytes 307216
  1086.8 23.6 %reduce-scatter.32.cloned.1.call-done = f32[240,120]{1,0:T(8,128)} async-done(((f32[960,120]{1,0:T(8,128)}), f32[240,120]{1,0:T(8,128)}) %reduce-scatter.32.cloned.1.call-update) | async-done | bytes 115216 | tf_op jit(solution)/shard_map/reduce_scatter | solution.py:280
  1110.3 26.6 %reduce-scatter.34.cloned.1.call-done = f32[400,120]{1,0:T(8,128)} async-done(((f32[1600,120]{1,0:T(8,128)}), f32[400,120]{1,0:T(8,128)}) %reduce-scatter.34.cloned.1.call-update) | async-done | bytes 192016
  (249 shorter events, 353.1 us)
Async XLA Ops:
  7.2 66.5 %all-gather.12.cloned.1.call-start = ((), (), s32[]{:S(2)}) async-start(), calls=%async_computation.11 | async-start | bytes 4096000 | tf_op jit(solution)/shard_map/all_gather | solution.py:143
  43.4 75.0 %all-gather.16.cloned.1.call-start = ((), (), s32[]{:S(2)}) async-start(), calls=%async_computation.13 | async-start | bytes 1638400 | tf_op jit(solution)/shard_map/all_gather | solution.py:169
  80.1 38.7 %all-gather.14.cloned.1.call-start = ((), (), s32[]{:S(2)}) async-start(), calls=%async_computation.12 | async-start | bytes 1638400 | tf_op jit(solution)/shard_map/all_gather | solution.py:168
  82.6 152.2 %all-gather.18.cloned.1.call-start = ((), (), s32[]{:S(2)}) async-start(), calls=%async_computation.14 | async-start | bytes 2457600 | tf_op jit(solution)/shard_map/all_gather | solution.py:144
  115.2 163.3 %all-gather.24.cloned.1.call-start = ((), (), s32[]{:S(2)}) async-start(), calls=%async_computation.17 | async-start | bytes 1382400 | tf_op jit(solution)/shard_map/all_gather | solution.py:138
  115.8 162.7 %all-gather.28.cloned.1.call-start = ((), (), s32[]{:S(2)}) async-start(), calls=%async_computation.24 | async-start | bytes 4915200 | tf_op jit(solution)/shard_map/all_gather | solution.py:220
  116.4 170.8 %all-gather.22.cloned.1.call-start = ((), (), s32[]{:S(2)}) async-start(), calls=%async_computation.16 | async-start | bytes 1382400 | tf_op jit(solution)/shard_map/all_gather | solution.py:137
  117.2 189.5 %all-gather.20.cloned.1.call-start = ((), (), s32[]{:S(2)}) async-start(), calls=%async_computation.15 | async-start | bytes 4915200 | tf_op jit(solution)/shard_map/all_gather | solution.py:190
  240.0 110.3 %all-gather.26.cloned.1.call-start = ((), (), s32[]{:S(2)}) async-start(), calls=%async_computation.19 | async-start | bytes 1382400 | tf_op jit(solution)/shard_map/all_gather | solution.py:206
  240.0 10.0 collective-permute-start
  241.5 11.7 %collective-permute-start.1 = (bf16[120,640]{1,0:T(8,128)(2,1)S(1)}, bf16[120,640]{1,0:T(8,128)(2,1)}, u32[]{:S(2)}, u32[]{:S(2)}) collective-permute-start(bf16[120,640]{1,0:T(8,128)(2,1)S(1)} %copy-done.13), channel_id=1, source_target_pairs={{0,28},{4,0},{8,4},{12,8},{16,12},{20,16},{24,20},{28,24},{1,29},{... | collective-permute-start | bytes 460808 | tf_op jit(solution)/shard_map/ppermute | solution.py:29
  244.8 184.5 %reduce-scatter.26.cloned.1.call-start = ((), (), s32[]{:S(2)}) async-start(), calls=%async_computation.20 | async-start | bytes 9830400 | tf_op jit(solution)/shard_map/reduce_scatter | solution.py:227
  250.0 11.6 %collective-permute-start.2 = (bf16[120,640]{1,0:T(8,128)(2,1)}, bf16[120,640]{1,0:T(8,128)(2,1)S(1)}, u32[]{:S(2)}, u32[]{:S(2)}) collective-permute-start(bf16[120,640]{1,0:T(8,128)(2,1)} %collective-permute-done), channel_id=1, source_target_pairs={{0,4},{4,8},{8,12},{12,16},{16,20},{20,24},{24,28},{28,0},{1,5},{5... | collective-permute-start | bytes 460808 | tf_op jit(solution)/shard_map/ppermute | solution.py:24
  253.2 10.9 collective-permute-start.3
  361.3 113.5 %reduce-scatter.24.cloned.1.call-start = ((), (), s32[]{:S(2)}) async-start(), calls=%async_computation.18 | async-start | bytes 4915200 | tf_op jit(solution)/shard_map/reduce_scatter | solution.py:196
  368.6 247.9 %reduce-scatter.30.cloned.1.call-start = ((), (), s32[]{:S(2)}) async-start(), calls=%async_computation.22 | async-start | bytes 3276800 | tf_op jit(solution)/shard_map/reduce_scatter | solution.py:250
  581.7 72.2 %reduce-scatter.28.cloned.1.call-start = ((), (), s32[]{:S(2)}) async-start(), calls=%async_computation.21 | async-start | bytes 3276800 | tf_op jit(solution)/shard_map/reduce_scatter | solution.py:249
  582.5 159.4 %reduce-scatter.36.cloned.1.call-start = ((), (), s32[]{:S(2)}) async-start(), calls=%async_computation.26 | async-start | bytes 4423680
  586.3 280.3 %reduce-scatter.38.cloned.1.call-start = ((), (), s32[]{:S(2)}) async-start(), calls=%async_computation.27 | async-start | bytes 7188480
  661.2 279.2 %reduce-scatter.44.cloned.1.call-start = ((), (), s32[]{:S(2)}) async-start(), calls=%async_computation.30 | async-start | bytes 2764800
  668.8 344.8 %reduce-scatter.40.cloned.1.call-start = ((), (), s32[]{:S(2)}) async-start(), calls=%async_computation.28 | async-start | bytes 2764800
  676.6 410.2 %reduce-scatter.42.cloned.1.call-start = ((), (), s32[]{:S(2)}) async-start(), calls=%async_computation.29 | async-start | bytes 2764800
  684.2 426.1 %reduce-scatter.32.cloned.1.call-start = ((), (), s32[]{:S(2)}) async-start(), calls=%async_computation.23 | async-start | bytes 614400 | tf_op jit(solution)/shard_map/reduce_scatter | solution.py:280
  744.0 393.0 %reduce-scatter.34.cloned.1.call-start = ((), (), s32[]{:S(2)}) async-start(), calls=%async_computation.25 | async-start | bytes 1024000
  (32 other events, 583.8 us)
Sparse Core Ops, SparseCore 0:
  43.5 30.1 all-gather.11
  80.2 18.1 all-gather.15
  100.6 18.1 all-gather.13
  120.8 21.8 all-gather.17
  144.7 41.4 all-gather.23
  187.6 31.7 all-gather.27
  221.6 49.8 all-gather.21
  273.6 32.9 all-gather.19
  308.8 41.4 all-gather.25
  361.5 67.7 reduce-scatter.25
  432.0 42.8 reduce-scatter.23
  581.8 34.6 reduce-scatter.29
  619.2 34.6 reduce-scatter.27
  657.5 84.3 reduce-scatter.35
  745.8 120.7 reduce-scatter.37
  871.1 69.2 reduce-scatter.43
  944.9 68.7 reduce-scatter.39
  1018.1 68.6 reduce-scatter.41
  1090.0 20.2 reduce-scatter.31
  1113.5 23.4 reduce-scatter.33
